TPU v7x, 32 devices: a whole 2x2x4 slice. The times are simulated.
32 devices in a mesh: replica: 8 (over z, y), shard: 4 (over x, core).
Axes of the slice: x: 2, y: 2, z: 4, core: 2. Of those that a mesh axis runs over, the one named last changes fastest.
Arguments:
- block_input: bfloat16 [16, 256, 2048], P('replica', 'shard'), may hold values from -6 to 6
- segment_ids: int32 [16, 256], P('replica'), may hold values from 0 to 3, never falling along the last dimension, each value on 1 to 192 neighbouring positions
- norm_gain: bfloat16 [2048], P('shard'), may hold values from 0.5 to 1.5
- w_in: bfloat16 [2048, 8192], P(None, 'shard'), may hold values from -0.125 to 0.125
- conv_weight: bfloat16 [4, 4096], P(None, 'shard'), may hold values from -3 to 3
- conv_bias: bfloat16 [4096], P('shard'), may hold values from -1.5 to 1.5
- x_proj: bfloat16 [160, 4096], P(None, 'shard'), may hold values from -1 to 1
- dt_proj: bfloat16 [128, 4096], P(None, 'shard'), may hold values from -0.5 to 0.5
- dt_bias: bfloat16 [4096], P('shard'), may hold values from -4 to 1
- d_skip: bfloat16 [4096], P('shard'), may hold values from 0.5 to 1.5
- out_proj: bfloat16 [4096, 2048], P(None, 'shard'), may hold values from -0.1875 to 0.1875
- out_grad: bfloat16 [16, 256, 2048], P('replica', 'shard'), may hold values from -6 to 6
Outputs:
- block_output: bfloat16 [16, 256, 2048], P('replica', 'shard')
- input_grad: bfloat16 [16, 256, 2048], P('replica', 'shard')
- grad_norm_gain: float32 [2048], P('shard')
- grad_w_in: float32 [2048, 8192], P('replica', 'shard')
- grad_conv_weight: float32 [4, 4096], P(None, 'shard')
- grad_conv_bias: float32 [4096], P('shard')
- grad_x_proj: float32 [160, 4096], P(None, 'shard')
- grad_dt_proj: float32 [128, 4096], P(None, 'shard')
- grad_dt_bias: float32 [4096], P('shard')
- grad_d_skip: float32 [4096], P('shard')
- grad_out_proj: float32 [4096, 2048], P('replica', 'shard')
Inputs may be any that keep to these rules, and one draw needn't show every extreme that they name: `segment_ids`: within each sequence the ids never fall; each of the 4 documents holds 1 to 192 tokens and one holds exactly 192.
All inputs are finite; a program needn't handle non-finite values.
Results may differ from a plain program's by a relative error of at most 0.012.
The roundings to bfloat16 on the way count: a program that leaves them out, or rounds other values in their place, can miss the bound.
Values may be sent and summed in bfloat16 or wider, within the bound.
A program may use at most 240 MiB of HBM per device.

v0:
```python
import jax
import jax.numpy as jnp
from jax import lax
from jax.sharding import PartitionSpec as P

KW = 4
EPS = 1e-05
block_len = 16


def passed_along(block, axis, distance):
    devices = range(lax.axis_size(axis))
    route = [(i - distance, i) for i in devices if i - distance in devices]
    return lax.ppermute(block, axis, route)


def carried_in(value, axis, join, neutral):
    count, mine = (lax.axis_size(axis), lax.axis_index(axis))
    pieces = jax.tree.map(lambda part: lax.all_gather(part, axis), value)
    total = jax.tree.map(
        lambda part, zero: jnp.full_like(part, 0) + jnp.asarray(zero, part.dtype), value, neutral
    )

    def hop(position, total):
        longer = join(total, jax.tree.map(lambda part: part[position], pieces))
        return jax.tree.map(lambda new, old: jnp.where(position < mine, new, old), longer, total)

    return lax.fori_loop(0, count - 1, hop, total)


def entering(shard, axis, join, neutral):
    count = lax.axis_size(axis)
    place = lax.axis_index(axis)
    ahead = count - 1 - place
    gathered = jax.tree.map(
        lambda a, kind: lax.all_gather(a.astype(kind), axis), shard, (jnp.bfloat16, jnp.bfloat16)
    )
    state = jax.tree.map(lambda a, e: jnp.zeros_like(a) + jnp.asarray(e, a.dtype), shard, neutral)

    def one(hop, state):
        source = count - 1 - hop
        return join(
            state,
            jax.tree.map(
                lambda a, own: lax.dynamic_index_in_dim(a, source, 0, False).astype(own.dtype),
                gathered,
                shard,
            ),
        )

    return lax.fori_loop(0, ahead, one, state)


def rows_dot(first_op, second_op):
    return jnp.dot(first_op, second_op, preferred_element_type=jnp.float32)


def inner_dot(first_op, second_op):
    return lax.dot_general(
        first_op, second_op, (((0,), (0,)), ((), ())), preferred_element_type=jnp.float32
    )


def outer_dot(first_op, second_op):
    return lax.dot_general(
        first_op, second_op, (((1,), (1,)), ((), ())), preferred_element_type=jnp.float32
    )


def silu_slope(values):
    sig_val = jax.nn.sigmoid(values)
    return sig_val + values * sig_val * (1.0 - sig_val)


def decay_of(rate_row, key_row, keep_val):
    return (1.0 - rate_row[:, None] * (key_row * key_row)[None, :]) * keep_val


def block_forward(carried, pieces):
    rate_blk, conv_blk, key_blk, query_blk, keep_blk = pieces
    outputs = []
    for t in range(rate_blk.shape[0]):
        decay_now = decay_of(rate_blk[t], key_blk[t], keep_blk[t])
        carried = decay_now * carried + (rate_blk[t] * conv_blk[t])[:, None] * key_blk[t][None, :]
        outputs.append(jnp.sum(carried * query_blk[t][None, :], axis=1))
    return (carried, jnp.stack(outputs))


def block_product(carried, pieces):
    total_decay, local_state = carried
    rate_blk, conv_blk, key_blk, query_blk, keep_blk = pieces
    for t in range(rate_blk.shape[0]):
        decay_now = decay_of(rate_blk[t], key_blk[t], keep_blk[t])
        total_decay = decay_now * total_decay
        local_state = (
            decay_now * local_state + (rate_blk[t] * conv_blk[t])[:, None] * key_blk[t][None, :]
        )
    return ((total_decay, local_state), None)


def block_record(carried, pieces):
    end_state, outputs = block_forward(carried, pieces)
    return (end_state, (carried, outputs))


def block_adjoint(adjoint, pieces):
    rate_blk, key_blk, query_blk, keep_blk, dout_blk = pieces
    for t in reversed(range(rate_blk.shape[0])):
        adjoint = adjoint + dout_blk[t][:, None] * query_blk[t][None, :]
        adjoint = decay_of(rate_blk[t], key_blk[t], keep_blk[t]) * adjoint
    return (adjoint, None)


def block_backward(grad_state, inputs):
    start_state = inputs[0]
    pieces = inputs[1:6]
    dout_blk = inputs[6]
    pullback = jax.vjp(block_forward, start_state, pieces)[1]
    grad_start, grad_pieces = pullback((grad_state, dout_blk))
    return (grad_start, grad_pieces[:4])


def chain_combine(earlier, later):
    return (earlier[0] * later[0], later[0] * earlier[1] + later[1])


def conv_apply(extended, conv_w, conv_b, tap_masks):
    tok_local = extended.shape[0] - (KW - 1)
    conv_sum = conv_b + conv_w[KW - 1] * extended[KW - 1 :]
    for j in range(KW - 1):
        conv_sum = (
            conv_sum + conv_w[j] * extended[j : j + tok_local] * tap_masks[KW - 2 - j][:, None]
        )
    return conv_sum


def one_batch(weights, x_rows, cot_rows, seg_window):
    norm_gain, w_in, conv_weight, conv_bias, x_proj, dt_proj, dt_bias, d_skip, out_proj = weights
    tok_local = x_rows.shape[0]
    width = d_skip.shape[0]
    rank = dt_proj.shape[0]
    state_dim = (x_proj.shape[0] - rank) // 2
    count_blocks = tok_local // block_len
    x_vals = x_rows.astype(jnp.float32)
    inv_rms = lax.rsqrt(jnp.mean(x_vals * x_vals, axis=1, keepdims=True) + EPS)
    gain_vals = norm_gain.astype(jnp.float32)
    normed = (x_vals * inv_rms * gain_vals).astype(jnp.bfloat16)
    mixed = rows_dot(normed, w_in).astype(jnp.bfloat16)
    x_part = mixed[:, :width]
    z_vals = mixed[:, width:].astype(jnp.float32)
    edge_rows = passed_along(x_part[tok_local - (KW - 1) :], "shard", 1)
    extended = jnp.concatenate([edge_rows, x_part], axis=0).astype(jnp.float32)
    tap_masks = [
        (seg_window[KW - 1 - d : KW - 1 - d + tok_local] == seg_window[KW - 1 :]).astype(
            jnp.float32
        )
        for d in range(1, KW)
    ]
    keep_rows = tap_masks[0]
    conv_w = conv_weight.astype(jnp.float32)
    conv_b = conv_bias.astype(jnp.float32)
    conv_pre = conv_apply(extended, conv_w, conv_b, tap_masks)
    conv_out = jax.nn.silu(conv_pre).astype(jnp.bfloat16)
    conv_vals = conv_out.astype(jnp.float32)
    proj_vals = outer_dot(conv_out, x_proj)
    dt_low = proj_vals[:, :rank].astype(jnp.bfloat16)
    key_rows = proj_vals[:, rank : rank + state_dim]
    query_rows = proj_vals[:, rank + state_dim :]
    beta_vals = jax.nn.sigmoid(rows_dot(dt_low, dt_proj) + dt_bias.astype(jnp.float32))
    key_square = jnp.sum(key_rows * key_rows, axis=1, keepdims=True)
    denom_inv = 1.0 / (1.0 + beta_vals * key_square)
    step_rate = beta_vals * denom_inv

    def blocked(values):
        return values.reshape((count_blocks, block_len) + values.shape[1:])

    pieces = (
        blocked(step_rate),
        blocked(conv_vals),
        blocked(key_rows),
        blocked(query_rows),
        blocked(keep_rows),
    )
    unit_state = jnp.ones((width, state_dim), jnp.float32)
    zero_state = jnp.zeros((width, state_dim), jnp.float32)
    total_decay, local_state = lax.scan(block_product, (unit_state, zero_state), pieces)[0]
    state_in = carried_in(
        (total_decay, local_state), "shard", chain_combine, (unit_state, zero_state)
    )[1]
    starts, rec_blocks = lax.scan(block_record, state_in, pieces)[1]
    recurrent = rec_blocks.reshape(tok_local, width)
    skip_vals = d_skip.astype(jnp.float32)
    y_total = recurrent + skip_vals * conv_vals
    gate_act = jax.nn.silu(z_vals)
    gated = (y_total * gate_act).astype(jnp.bfloat16)
    out_val = (x_vals + rows_dot(gated, out_proj)).astype(jnp.bfloat16)
    grad_out_proj = inner_dot(gated, cot_rows)
    grad_gated = outer_dot(cot_rows, out_proj)
    grad_y = grad_gated * gate_act
    grad_z = grad_gated * y_total * silu_slope(z_vals)
    grad_d_skip = jnp.sum(grad_y * conv_vals, axis=0)
    dout_blocks = blocked(grad_y)
    adj_pieces = (pieces[0], pieces[2], pieces[3], pieces[4], dout_blocks)
    grad_local = lax.scan(block_adjoint, zero_state, adj_pieces, reverse=True)[0]
    grad_end = entering(
        (total_decay, grad_local), "shard", chain_combine, (unit_state, zero_state)
    )[1]
    back_pieces = (starts,) + pieces + (dout_blocks,)
    rate_back, conv_back, key_back, query_back = lax.scan(
        block_backward, grad_end, back_pieces, reverse=True
    )[1]
    grad_rate = rate_back.reshape(tok_local, width)
    grad_keys = key_back.reshape(tok_local, state_dim)
    grad_queries = query_back.reshape(tok_local, state_dim)
    grad_conv = grad_y * skip_vals + conv_back.reshape(tok_local, width)
    grad_keys = grad_keys - 2.0 * key_rows * jnp.sum(
        grad_rate * step_rate * step_rate, axis=1, keepdims=True
    )
    grad_dt = grad_rate * denom_inv * denom_inv * beta_vals * (1.0 - beta_vals)
    grad_dt_bias = jnp.sum(grad_dt, axis=0)
    grad_dt_low = grad_dt.astype(jnp.bfloat16)
    grad_dt_proj = inner_dot(dt_low, grad_dt_low)
    grad_dt_in = outer_dot(grad_dt_low, dt_proj)
    grad_proj = jnp.concatenate([grad_dt_in, grad_keys, grad_queries], axis=1).astype(jnp.bfloat16)
    grad_x_proj = inner_dot(grad_proj, conv_out)
    grad_conv = grad_conv + rows_dot(grad_proj, x_proj)
    grad_pre = grad_conv * silu_slope(conv_pre)

    def conv_local(ext_vals, tap_wts, bias_vals):
        return conv_apply(ext_vals, tap_wts, bias_vals, tap_masks)

    conv_pull = jax.vjp(conv_local, extended, conv_w, conv_b)[1]
    grad_ext, grad_conv_weight, grad_conv_bias = conv_pull(grad_pre)
    back_rows = passed_along(grad_ext[: KW - 1].astype(jnp.bfloat16), "shard", -1).astype(
        jnp.float32
    )
    grad_x_part = jnp.concatenate(
        [grad_ext[KW - 1 : tok_local], grad_ext[tok_local:] + back_rows], axis=0
    )
    grad_mixed = jnp.concatenate([grad_x_part, grad_z], axis=1).astype(jnp.bfloat16)
    grad_w_in = inner_dot(normed, grad_mixed)
    grad_normed = outer_dot(grad_mixed, w_in)
    grad_norm_gain = jnp.sum(grad_normed * x_vals * inv_rms, axis=0)
    scaled = grad_normed * gain_vals
    grad_x = inv_rms * (
        scaled - x_vals * inv_rms * inv_rms * jnp.mean(scaled * x_vals, axis=1, keepdims=True)
    )
    dx_val = (cot_rows.astype(jnp.float32) + grad_x).astype(jnp.bfloat16)
    grad_list = (
        grad_norm_gain,
        grad_w_in,
        grad_conv_weight,
        grad_conv_bias,
        grad_x_proj,
        grad_dt_proj,
        grad_dt_bias,
        grad_d_skip,
        grad_out_proj,
    )
    return (out_val, dx_val, grad_list)


def body(
    block_input,
    segment_ids,
    norm_gain,
    w_in,
    conv_weight,
    conv_bias,
    x_proj,
    dt_proj,
    dt_bias,
    d_skip,
    out_proj,
    out_grad,
):
    micro_count = block_input.shape[0]
    tok_local = block_input.shape[1]
    shard_pos = lax.axis_index("shard")
    seg_padded = jnp.pad(segment_ids, ((0, 0), (KW - 1, 0)), constant_values=-1)
    seg_windows = lax.dynamic_slice_in_dim(seg_padded, shard_pos * tok_local, tok_local + KW - 1, 1)
    full_sums = None
    shard_sums = None
    out_rows = []
    grad_rows = []
    for m in range(micro_count):
        gathered = (
            lax.all_gather(norm_gain, "shard", axis=0, tiled=True),
            lax.all_gather(w_in, "shard", axis=1, tiled=True),
            lax.all_gather(conv_weight, "shard", axis=1, tiled=True),
            lax.all_gather(conv_bias, "shard", axis=0, tiled=True),
            lax.all_gather(x_proj, "shard", axis=1, tiled=True),
            lax.all_gather(dt_proj, "shard", axis=1, tiled=True),
            lax.all_gather(dt_bias, "shard", axis=0, tiled=True),
            lax.all_gather(d_skip, "shard", axis=0, tiled=True),
            lax.all_gather(out_proj, "shard", axis=1, tiled=True),
        )
        out_val, dx_val, grad_list = one_batch(
            gathered, block_input[m], out_grad[m], seg_windows[m]
        )
        out_rows.append(out_val)
        grad_rows.append(dx_val)
        full_sums = (
            grad_list if full_sums is None else tuple((a + b for a, b in zip(full_sums, grad_list)))
        )
    shard_sums = (
        lax.psum_scatter(
            full_sums[0].astype(jnp.bfloat16), "shard", scatter_dimension=0, tiled=True
        ).astype(jnp.float32),
        lax.psum_scatter(
            full_sums[1].astype(jnp.bfloat16), "shard", scatter_dimension=1, tiled=True
        ).astype(jnp.float32),
        lax.psum_scatter(
            full_sums[2].astype(jnp.bfloat16), "shard", scatter_dimension=1, tiled=True
        ).astype(jnp.float32),
        lax.psum_scatter(
            full_sums[3].astype(jnp.bfloat16), "shard", scatter_dimension=0, tiled=True
        ).astype(jnp.float32),
        lax.psum_scatter(
            full_sums[4].astype(jnp.bfloat16), "shard", scatter_dimension=1, tiled=True
        ).astype(jnp.float32),
        lax.psum_scatter(
            full_sums[5].astype(jnp.bfloat16), "shard", scatter_dimension=1, tiled=True
        ).astype(jnp.float32),
        lax.psum_scatter(
            full_sums[6].astype(jnp.bfloat16), "shard", scatter_dimension=0, tiled=True
        ).astype(jnp.float32),
        lax.psum_scatter(
            full_sums[7].astype(jnp.bfloat16), "shard", scatter_dimension=0, tiled=True
        ).astype(jnp.float32),
        lax.psum_scatter(
            full_sums[8].astype(jnp.bfloat16), "shard", scatter_dimension=1, tiled=True
        ).astype(jnp.float32),
    )
    large_sums = (
        lax.psum_scatter(shard_sums[1], "replica", scatter_dimension=0, tiled=True),
        lax.psum_scatter(shard_sums[8], "replica", scatter_dimension=0, tiled=True),
    )
    small_sums = lax.psum(
        (
            shard_sums[0],
            shard_sums[2],
            shard_sums[3],
            shard_sums[4],
            shard_sums[5],
            shard_sums[6],
            shard_sums[7],
        ),
        "replica",
    )
    return (
        jnp.stack(out_rows),
        jnp.stack(grad_rows),
        small_sums[0],
        large_sums[0],
        small_sums[1],
        small_sums[2],
        small_sums[3],
        small_sums[4],
        small_sums[5],
        small_sums[6],
        large_sums[1],
    )


def solution(mesh):
    return jax.shard_map(
        body,
        mesh=mesh,
        in_specs=(
            P("replica", "shard", None),
            P("replica", None),
            P("shard"),
            P(None, "shard"),
            P(None, "shard"),
            P("shard"),
            P(None, "shard"),
            P(None, "shard"),
            P("shard"),
            P("shard"),
            P(None, "shard"),
            P("replica", "shard", None),
        ),
        out_specs=(
            P("replica", "shard", None),
            P("replica", "shard", None),
            P("shard"),
            P("replica", "shard"),
            P(None, "shard"),
            P("shard"),
            P(None, "shard"),
            P(None, "shard"),
            P("shard"),
            P("shard"),
            P("replica", "shard"),
        ),
        check_vma=False,
    )
```

profile of v0, /device:TPU:0, one launch (start us, length us, event | category | flops | bytes accessed | tf_op | source)
XLA Modules:
  0.0 2360.5 jit_solution(17861980219472843263)
XLA Ops:
  42.2 171.9 %all-gather.18.cloned.1.call-done = bf16[2048,8192]{1,0:T(8,128)(2,1)} async-done(((bf16[2048,2048]{1,0:T(8,128)(2,1)}), bf16[2048,8192]{1,0:T(8,128)(2,1)}) %all-gather.18.cloned.1.call-update) | async-done | bytes 33554448 | tf_op jit(solution)/shard_map/all_gather | solution.py:289
  214.1 15.5 convolution_convert_fusion.1
  231.8 14.6 convolution_convert_fusion
  252.0 69.6 %all-gather.24.cloned.1.call-done = bf16[4096,2048]{1,0:T(8,128)(2,1)} async-done(((bf16[4096,512]{1,0:T(8,128)(2,1)}), bf16[4096,2048]{1,0:T(8,128)(2,1)}) %all-gather.24.cloned.1.call-update) | async-done | bytes 16777232 | tf_op jit(solution)/shard_map/all_gather | solution.py:296
  321.6 15.2 multiply_reduce_fusion.193
  345.4 14.9 all-gather.22.cloned.1.call-done
  363.1 102.7 %while.190 = (s32[]{:T(128)}, f32[4096,16]{0,1:T(8,128)S(1)}, f32[4096,16]{0,1:T(8,128)}, f32[4,16,4096]{2,1,0:T(8,128)S(1)}, f32[4,16,16]{2,1,0:T(8,128)}, /*in...) while((s32[]{:T(128)}, f32[4096,16]{0,1:T(8,128)S(1)}, ...), condition=%wide.region_3.4_spmd.clone, body=%wide.region_2.3_spmd.clone.sunk | while | flops 10682642 | bytes 5774296 | solution.py:186
  366.7 11.3 multiply_add_fusion.148
  378.0 10.8 fusion.699
  392.3 11.3 multiply_add_fusion.148
  403.6 10.8 fusion.699
  418.0 11.3 multiply_add_fusion.148
  429.3 10.8 fusion.699
  443.7 11.3 multiply_add_fusion.148
  455.0 10.8 fusion.699
  468.5 15.7 multiply_reduce_fusion.192
  489.1 102.7 %while.192 = (s32[]{:T(128)}, f32[4096,16]{0,1:T(8,128)S(1)}, f32[4096,16]{0,1:T(8,128)S(1)}, f32[4,16,4096]{2,1,0:T(8,128)S(1)}, f32[4,16,16]{2,1,0:T(8,128)S(1...) while((s32[]{:T(128)}, f32[4096,16]{0,1:T(8,128)S(1)}, ...), condition=%wide.region_27.28_spmd.clone, body=%wide.region_26.27_spmd.clone.sunk | while | flops 10682642 | bytes 3677088 | solution.py:186
  493.0 11.2 multiply_add_fusion.149
  504.2 10.7 fusion.703
  518.8 11.2 multiply_add_fusion.149
  544.5 11.2 multiply_add_fusion.149
  570.0 11.2 multiply_add_fusion.149
  592.6 65.8 %while.194 = (s32[]{:T(128)}, f32[4096,16]{0,1:T(8,128)S(1)}, f32[4,16,4096]{2,1,0:T(8,128)S(1)}, f32[4,16,16]{2,1,0:T(8,128)}, f32[4,16]{1,0:T(4,128)}, /*index...) while((s32[]{:T(128)}, f32[4096,16]{0,1:T(8,128)S(1)}, ...), condition=%wide.region_49.50_spmd.clone, body=%wide.region_48.49_spmd.clone.sunk | while | flops 6357267 | bytes 2104179 | solution.py:204
  597.8 11.2 add_multiply_fusion.4
  614.3 11.2 add_multiply_fusion.4
  630.8 11.2 add_multiply_fusion.4
  647.2 11.2 add_multiply_fusion.4
  679.0 60.7 %while.195 = (s32[]{:T(128)}, f32[4096,16]{0,1:T(8,128)S(1)}, f32[4,16,4096]{2,1,0:T(8,128)S(1)}, f32[4,16,16]{2,1,0:T(8,128)S(1)}, f32[4,16]{1,0:T(4,128)S(1)},...) while((s32[]{:T(128)}, f32[4096,16]{0,1:T(8,128)S(1)}, ...), condition=%wide.region_137.138_spmd.clone, body=%wide.region_136.137_spmd.clone.sunk | while | flops 6357267 | bytes 2104179 | solution.py:204
  682.6 11.4 add_multiply_fusion.5
  698.1 11.4 add_multiply_fusion.5
  713.2 11.4 add_multiply_fusion.5
  728.2 11.4 add_multiply_fusion.5
  774.1 119.0 %while.184 = (s32[]{:T(128)}, f32[4096,16]{0,1:T(8,128)S(1)}, f32[4,4096,16]{1,2,0:T(8,128)}, f32[4,16,4096]{2,1,0:T(8,128)}, f32[4,16,4096]{2,1,0:T(8,128)S(1)}...) while((s32[]{:T(128)}, f32[4096,16]{0,1:T(8,128)S(1)}, ...), condition=%wide.region_23.24_spmd, body=%wide.region_6.23_spmd.sunk | while | flops 11534609 | bytes 8923085 | solution.py:190
  782.2 11.6 multiply_reduce_fusion.240
  811.8 11.6 multiply_reduce_fusion.240
  841.5 11.6 multiply_reduce_fusion.240
  871.4 11.6 multiply_reduce_fusion.240
  895.3 203.1 %while.187 = (s32[]{:T(128)}, f32[4096,16]{0,1:T(8,128)S(1)}, f32[4,16,4096]{2,1,0:T(8,128)}, f32[4,16,4096]{2,1,0:T(8,128)}, f32[4,16,16]{2,1,0:T(8,128)S(1)}, ...) while((s32[]{:T(128)}, f32[4096,16]{0,1:T(8,128)S(1)}, ...), condition=%wide.region_133.134_spmd, body=%wide.region_52.133_spmd.sunk | while | flops 34942480 | bytes 17066536 | solution.py:209
  903.1 11.3 multiply_add_fusion.146
  953.7 11.3 multiply_add_fusion.146
  1004.6 11.3 multiply_add_fusion.146
  1055.1 11.3 multiply_add_fusion.146
  1113.8 98.0 %while.185 = (s32[]{:T(128)}, f32[4096,16]{0,1:T(8,128)S(1)}, f32[4,4096,16]{1,2,0:T(8,128)}, f32[4,16,4096]{2,1,0:T(8,128)}, f32[4,16,4096]{2,1,0:T(8,128)S(1)}...) while((s32[]{:T(128)}, f32[4096,16]{0,1:T(8,128)S(1)}, ...), condition=%wide.region_47.48_spmd, body=%wide.region_30.47_spmd.sunk | while | flops 11534609 | bytes 8923085 | solution.py:190
  1119.4 12.0 multiply_reduce_fusion.249
  1143.9 12.0 multiply_reduce_fusion.249
  1168.4 12.0 multiply_reduce_fusion.249
  1192.7 12.0 multiply_reduce_fusion.249
  1213.9 195.1 %while.189 = (s32[]{:T(128)}, f32[4096,16]{0,1:T(8,128)S(1)}, f32[4,16,4096]{2,1,0:T(8,128)}, f32[4,16,4096]{2,1,0:T(8,128)}, f32[4,16,16]{2,1,0:T(8,128)S(1)}, ...) while((s32[]{:T(128)}, f32[4096,16]{0,1:T(8,128)S(1)}, ...), condition=%wide.region_221.222_spmd, body=%wide.region_140.221_spmd.sunk | while | flops 34942480 | bytes 17066536 | solution.py:209
  1218.9 11.7 multiply_add_fusion.147
  1268.0 11.7 multiply_add_fusion.147
  1316.7 11.7 multiply_add_fusion.147
  1365.4 11.7 multiply_add_fusion.147
  1415.6 13.6 fusion.432
  1429.1 18.9 add_convert_fusion.1
  1465.5 26.1 %fusion.425 = f32[2048,8192]{1,0:T(8,128)} fusion(bf16[64,4096]{1,0:T(8,128)(2,1)S(1)} %copy-done.18, bf16[3,4096]{1,0:T(4,128)(2,1)S(1)} %fusion.446, bf16[61,4096]{1,0:T(8,128)(2,1)S(1)} %slice.5298, f32[2048]{0:T(1024)S(1)} %bitcast.3490, f32[64]{0:T(128)S(1)} %copy-done.54, bf16[2,64,2048]{2,1,0:T(8,128)(2,1)S(1)} %copy-done.2), kind=kOutput, calls=%fused_computation.1561 | convolution fusion | flops 2151153664 | bytes 68461056 | tf_op jit(solution)/shard_map/dot_general | solution.py:59
  1491.6 33.7 %add_convert_fusion = bf16[2048,8192]{1,0:T(8,128)(2,1)} fusion(f32[2048,8192]{1,0:T(8,128)} %fusion.425, bf16[64,4096]{1,0:T(8,128)(2,1)S(1)} %copy-done.19, bf16[3,4096]{1,0:T(4,128)(2,1)S(1)} %fusion.445, bf16[61,4096]{1,0:T(8,128)(2,1)} %slice.5301, f32[64]{0:T(128)S(1)} %copy-done.52, f32[2048]{0:T(1024)S(1)} %bitcast.3491, ...), kind=kOutput, calls=%fused_computation.1428 | convolution fusion | flops 2184708096 | bytes 101990912 | tf_op jit(solution)/shard_map/dot_general | solution.py:59
  1536.4 38.0 %reduce-scatter.18.cloned.1.call-done = bf16[4096,512]{1,0:T(8,128)(2,1)} async-done(((bf16[4096,2048]{1,0:T(8,128)(2,1)}), bf16[4096,512]{1,0:T(8,128)(2,1)}) %reduce-scatter.18.cloned.1.call-update) | async-done | bytes 4194320 | tf_op jit(solution)/shard_map/reduce_scatter | solution.py:331
  1581.3 230.6 %reduce-scatter.10.cloned.1.call-done = bf16[2048,2048]{1,0:T(8,128)(2,1)} async-done(((bf16[2048,8192]{1,0:T(8,128)(2,1)}), bf16[2048,2048]{1,0:T(8,128)(2,1)}) %reduce-scatter.10.cloned.1.call-update) | async-done | bytes 8388624 | tf_op jit(solution)/shard_map/reduce_scatter | solution.py:310
  1811.9 11.6 convert_element_type.346
  1845.0 15.8 fusion.424
  1860.8 15.9 fusion.419
  1896.1 98.4 %all-reduce.216 = (f32[512]{0:T(512)}, f32[4,1024]{1,0:T(4,128)}, f32[1024]{0:T(1024)}, f32[160,1024]{1,0:T(8,128)}, f32[128,1024]{1,0:T(8,128)}, /*index=5*/f32[1024]{0:T(1024)}, f32[1024]{0:T(1024)}) all-reduce(f32[512]{0:T(512)S(1)} %dynamic-slice_convert_fusion.3, ...), channel_id=1, replica_groups=mesh['replica'=8,'shard'=4] {'replica'}, use_global_device_ids=true, to_apply=%region_227.228 | all-reduce | flops 302592 | bytes 1822720 | tf_op jit(solution)/shard_map/psum | solution.py:339
  1994.5 73.0 %reduce-scatter.20.cloned.1.call-done = f32[512,512]{1,0:T(8,128)} async-done(((f32[4096,512]{1,0:T(8,128)}), f32[512,512]{1,0:T(8,128)}) %reduce-scatter.20.cloned.1.call-update) | async-done | bytes 1048592 | tf_op jit(solution)/shard_map/reduce_scatter | solution.py:337
  2067.5 286.3 %reduce-scatter.12.cloned.1.call-done = f32[256,2048]{1,0:T(8,128)} async-done(((f32[2048,2048]{1,0:T(8,128)}), f32[256,2048]{1,0:T(8,128)}) %reduce-scatter.12.cloned.1.call-update) | async-done | bytes 2097168 | tf_op jit(solution)/shard_map/reduce_scatter | solution.py:336
  (1373 shorter events, 757.6 us)
Async XLA Ops:
  7.2 206.9 %all-gather.18.cloned.1.call-start = ((), (), s32[]{:S(2)}) async-start(), calls=%async_computation.7 | async-start | bytes 41943040 | tf_op jit(solution)/shard_map/all_gather | solution.py:289
  7.9 5.2 copy-start.82
  7.9 11.3 copy-start.75
  8.0 17.4 copy-start.76
  8.0 22.5 copy-start.77
  8.0 28.3 %copy-start.71 = (bf16[4,1024]{1,0:T(4,128)(2,1)S(1)}, bf16[4,1024]{1,0:T(4,128)(2,1)}, u32[]{:S(2)}) copy-start(bf16[4,1024]{1,0:T(4,128)(2,1)} %param.40) | copy-start | bytes 24580
  8.0 313.6 %all-gather.24.cloned.1.call-start = ((), (), s32[]{:S(2)}) async-start(), calls=%async_computation.10 | async-start | bytes 20971520 | tf_op jit(solution)/shard_map/all_gather | solution.py:296
  8.7 333.4 %all-gather.20.cloned.1.call-start = ((), (), s32[]{:S(2)}) async-start(), calls=%async_computation.8 | async-start | bytes 1638400 | tf_op jit(solution)/shard_map/all_gather | solution.py:292
  9.5 350.8 %all-gather.22.cloned.1.call-start = ((), (), s32[]{:S(2)}) async-start(), calls=%async_computation.9 | async-start | bytes 1310720 | tf_op jit(solution)/shard_map/all_gather | solution.py:293
  10.0 748.7 %all-gather.28.cloned.1.call-start = ((), (), s32[]{:S(2)}) async-start(), calls=%async_computation.18 | async-start | bytes 1310720 | tf_op jit(solution)/shard_map/all_gather | solution.py:19
  11.8 217.8 %copy-start.53 = (f32[64]{0:T(128)}, f32[64]{0:T(128)S(1)}, u32[]{:S(2)}) copy-start(f32[64]{0:T(128)S(1)} %add_rsqrt_fusion.1) | copy-start | bytes 772
  11.8 220.0 %copy-start.51 = (f32[64]{0:T(128)}, f32[64]{0:T(128)S(1)}, u32[]{:S(2)}) copy-start(f32[64]{0:T(128)S(1)} %add_rsqrt_fusion) | copy-start | bytes 772
  19.3 212.5 %copy-start.33 = (f32[4,1,512]{2,1,0:T(1,128)}, f32[4,1,512]{2,1,0:T(1,128)S(1)}, u32[]{:S(2)}) copy-start(f32[4,1,512]{2,1,0:T(1,128)S(1)} %convert_element_type.375) | copy-start | bytes 24580
  229.6 92.0 %copy-start.26 = (bf16[64,8192]{1,0:T(8,128)(2,1)}, bf16[64,8192]{1,0:T(8,128)(2,1)S(1)}, u32[]{:S(2)}) copy-start(bf16[64,8192]{1,0:T(8,128)(2,1)S(1)} %convolution_convert_fusion.1) | copy-start | bytes 3145732
  229.7 21.2 collective-permute-start
  246.5 75.2 %copy-start.30 = (bf16[2,64,2048]{2,1,0:T(8,128)(2,1)S(1)}, bf16[2,64,2048]{2,1,0:T(8,128)(2,1)}, u32[]{:S(2)}) copy-start(bf16[2,64,2048]{2,1,0:T(8,128)(2,1)} %param.47) | copy-start | bytes 1572868
  248.4 217.7 %collective-permute-start.1 = (bf16[3,4096]{1,0:T(4,128)(2,1)S(1)}, bf16[3,4096]{1,0:T(4,128)(2,1)S(1)}, u32[]{:S(2)}, u32[]{:S(2)}) collective-permute-start(bf16[3,4096]{1,0:T(4,128)(2,1)S(1)} %slice.5288), channel_id=1, source_target_pairs={{0,1},{1,2},{2,3},{4,5},{5,6},{6,7},{8,9},{9,10},{10,11},{12,13},{... | collective-permute-start | bytes 73736 | tf_op jit(solution)/shard_map/ppermute | solution.py:14
  336.9 23.4 copy-start.11
  344.0 19.1 copy-start.45
  363.1 105.4 %copy-start.59 = (f32[4096]{0:T(1024)S(1)}, f32[4096]{0:T(1024)}, u32[]{:S(2)}) copy-start(f32[4096]{0:T(1024)} %convert_element_type.292) | copy-start | bytes 49156
  363.1 105.4 %copy-start.64 = (f32[1,4096]{1,0:T(1,128)S(1)}, f32[1,4096]{1,0:T(1,128)}, u32[]{:S(2)}) copy-start(f32[1,4096]{1,0:T(1,128)} %get-tuple-element.3206) | copy-start | bytes 49156
  363.1 105.4 %copy-start.66 = (f32[1,4096]{1,0:T(1,128)S(1)}, f32[1,4096]{1,0:T(1,128)}, u32[]{:S(2)}) copy-start(f32[1,4096]{1,0:T(1,128)} %get-tuple-element.3207) | copy-start | bytes 49156
  363.1 105.4 %copy-start.68 = (f32[1,4096]{1,0:T(1,128)S(1)}, f32[1,4096]{1,0:T(1,128)}, u32[]{:S(2)}) copy-start(f32[1,4096]{1,0:T(1,128)} %get-tuple-element.3208) | copy-start | bytes 49156
  378.0 10.8 copy-start.10
  403.6 10.8 copy-start.10
  429.3 10.8 copy-start.10
  455.0 10.8 copy-start.10
  465.8 18.4 copy-start
  465.8 18.3 copy-start.4
  465.8 295.8 %all-gather.26.cloned.1.call-start = ((), (), s32[]{:S(2)}) async-start(), calls=%async_computation.17 | async-start | bytes 1310720 | tf_op jit(solution)/shard_map/all_gather | solution.py:19
  591.9 86.1 %copy-start.3 = (f32[4096,16]{0,1:T(8,128)}, f32[4096,16]{0,1:T(8,128)S(1)}, u32[]{:S(2)}) copy-start(f32[4096,16]{0,1:T(8,128)S(1)} %get-tuple-element.1341) | copy-start | bytes 786436
  591.9 506.5 %all-gather.32.cloned.1.call-start = ((), (), s32[]{:S(2)}) async-start(), calls=%async_computation.20 | async-start | bytes 1310720 | tf_op jit(solution)/shard_map/all_gather | solution.py:19
  592.6 65.8 %copy-start.5 = (f32[4096,16]{0,1:T(8,128)S(1)}, f32[4096,16]{0,1:T(8,128)}, u32[]{:S(2)}) copy-start(f32[4096,16]{0,1:T(8,128)} %copy-done.4) | copy-start | bytes 786436
  674.6 426.8 %all-gather.30.cloned.1.call-start = ((), (), s32[]{:S(2)}) async-start(), calls=%async_computation.19 | async-start | bytes 1310720 | tf_op jit(solution)/shard_map/all_gather | solution.py:19
  674.7 4.3 copy-start.6
  678.7 895.7 %reduce-scatter.18.cloned.1.call-start = ((), (), s32[]{:S(2)}) async-start(), calls=%async_computation.15 | async-start | bytes 20971520 | tf_op jit(solution)/shard_map/reduce_scatter | solution.py:331
  739.6 15.7 copy-start.35
  739.7 15.7 copy-start.41
  739.7 15.7 copy-start.80
  1213.9 195.1 %copy-start.12 = (bf16[64,4096]{1,0:T(8,128)(2,1)S(1)}, bf16[64,4096]{1,0:T(8,128)(2,1)}, u32[]{:S(2)}) copy-start(bf16[64,4096]{1,0:T(8,128)(2,1)} %copy-done.11) | copy-start | bytes 1572868
  1213.9 195.1 %copy-start.50 = (f32[4096]{0:T(1024)S(1)}, f32[4096]{0:T(1024)}, u32[]{:S(2)}) copy-start(f32[4096]{0:T(1024)} %convert_element_type.309) | copy-start | bytes 49156
  1409.1 6.5 copy-start.31
  1415.6 13.6 copy-start.15
  1448.1 363.8 %reduce-scatter.10.cloned.1.call-start = ((), (), s32[]{:S(2)}) async-start(), calls=%async_computation.11 | async-start | bytes 41943040 | tf_op jit(solution)/shard_map/reduce_scatter | solution.py:310
  1448.7 4.2 copy-start.37
  1452.3 5.1 copy-start.23
  1455.7 7.4 collective-permute-start.2
  1460.7 4.8 copy-start.2
  1460.7 4.8 copy-start.18
  1460.7 4.7 copy-start.34
  1460.7 4.7 copy-start.54
  1460.9 30.8 %copy-start.20 = (bf16[61,4096]{1,0:T(8,128)(2,1)}, bf16[61,4096]{1,0:T(8,128)(2,1)S(1)}, u32[]{:S(2)}) copy-start(bf16[61,4096]{1,0:T(8,128)(2,1)S(1)} %slice.5298) | copy-start | bytes 1499140
  1461.8 3.6 collective-permute-start.3
  1465.5 26.1 %copy-start.19 = (bf16[64,4096]{1,0:T(8,128)(2,1)S(1)}, bf16[64,4096]{1,0:T(8,128)(2,1)}, u32[]{:S(2)}) copy-start(bf16[64,4096]{1,0:T(8,128)(2,1)} %get-tuple-element.3213) | copy-start | bytes 1572868
  1465.5 26.1 %copy-start.52 = (f32[64]{0:T(128)S(1)}, f32[64]{0:T(128)}, u32[]{:S(2)}) copy-start(f32[64]{0:T(128)} %copy-done.51) | copy-start | bytes 772
  1525.4 363.1 %reduce-scatter.22.cloned.1.call-start = ((), (), s32[]{:S(2)}) async-start(), calls=%async_computation.21 | async-start | bytes 1310720
  1530.6 359.0 %reduce-scatter.16.cloned.1.call-start = ((), (), s32[]{:S(2)}) async-start(), calls=%async_computation.14 | async-start | bytes 1310720 | tf_op jit(solution)/shard_map/reduce_scatter | solution.py:322
  1533.7 362.4 %reduce-scatter.14.cloned.1.call-start = ((), (), s32[]{:S(2)}) async-start(), calls=%async_computation.13 | async-start | bytes 1638400 | tf_op jit(solution)/shard_map/reduce_scatter | solution.py:319
  1536.4 531.2 %reduce-scatter.20.cloned.1.call-start = ((), (), s32[]{:S(2)}) async-start(), calls=%async_computation.16 | async-start | bytes 9437184 | tf_op jit(solution)/shard_map/reduce_scatter | solution.py:337
  1581.1 772.8 %reduce-scatter.12.cloned.1.call-start = ((), (), s32[]{:S(2)}) async-start(), calls=%async_computation.12 | async-start | bytes 18874368 | tf_op jit(solution)/shard_map/reduce_scatter | solution.py:336
  1826.1 9.1 copy-start.16
  1835.2 9.8 copy-start.22
  1845.0 15.8 copy-start.21
  1860.8 26.4 %copy-start.32 = (bf16[2,64,2048]{2,1,0:T(8,128)(2,1)S(1)}, bf16[2,64,2048]{2,1,0:T(8,128)(2,1)}, u32[]{:S(2)}) copy-start(bf16[2,64,2048]{2,1,0:T(8,128)(2,1)} %param.47) | copy-start | bytes 1572868
  (53 other events, 137.8 us)
Sparse Core Ops, SparseCore 0:
  9.6 204.4 all-gather.17
  215.7 105.9 all-gather.23
  323.2 18.8 all-gather.19
  343.5 16.7 all-gather.21
  466.0 16.7 all-gather.27
  592.0 16.7 all-gather.25
  674.7 16.7 all-gather.31
  693.1 16.7 all-gather.29
  1448.2 126.1 reduce-scatter.17
  1577.0 234.8 reduce-scatter.9
  1814.6 24.8 reduce-scatter.21
  1841.9 24.8 reduce-scatter.15
  1869.5 26.5 reduce-scatter.13
  1900.2 167.2 reduce-scatter.19
  2072.2 281.5 reduce-scatter.11
where the time goes:
time: 2380 us; the launch traced here: 2360 us
  waiting for transfers between devices  901 us (38%)
  other arithmetic  841 us (35%)
  matrix products  225 us (9%)
  local copies, waits for them, and re-layouts  197 us (8%)
  blocking collectives  164 us (7%)
    reduce_scatter x1, waiting for transfers between devices, body(): lax.psum_scatter(shard_sums[1], 'replica', scatter_dimension=0, tiled=True)  286 us
    reduce_scatter x1, waiting for transfers between devices, body(): lax.psum_scatter(full_sums[1].astype(jnp.bfloat16), 'shard', scatter_dime...  231 us
    reduce_sum x72, other arithmetic, decay_of(): return (1.0 - rate_row[:, None] * (key_row * key_row)[None, :]) * keep_val  219 us
    all_gather x1, waiting for transfers between devices, body(): lax.all_gather(w_in, 'shard', axis=1, tiled=True)  172 us
    reduce_sum x72, other arithmetic, block_forward(): outputs.append(jnp.sum(carried * query_blk[t][None, :], axis=1))  157 us
    dot_general x8, matrix products, inner_dot(): lax.dot_general(first_op, second_op, (((0,), (0,)), ((), ())), preferred_...  100 us
    psum x1, blocking collectives, body(): lax.psum((shard_sums[0], shard_sums[2], shard_sums[3], shard_sums[4], sha...  98.4 us
    add x8, other arithmetic, block_forward(): decay_now * carried  92.3 us
  transfers between devices with their start and end apart: 19, of which 10 were waited for; matrix products, arithmetic and copies ran while one was open for 39% of the time, Pallas kernels for 0%

commit v1 on v0

--- a/solution.py
+++ b/solution.py
@@ -284,9 +284,39 @@
     out_rows = []
     grad_rows = []
     for m in range(micro_count):
+
+        def prepare_forms(frame_in, lane_axis):
+            response = jax.lax.axis_size(lane_axis)
+            extra = jax.lax.axis_index(lane_axis)
+            lower, w2, opened = (response, extra, frame_in.shape[1])
+            all_rows = tuple((ix * lower if w == 1 else ix for w, ix in enumerate(frame_in.shape)))
+            n_now = lax.dynamic_update_slice_in_dim(
+                jnp.zeros(all_rows, frame_in.dtype), frame_in, w2 * opened, axis=1
+            )
+            arr_out = even = frame_in
+            for dev_i in range(1, lower // 2 + 1):
+                arr_out = jax.lax.ppermute(
+                    arr_out,
+                    axis_name=lane_axis,
+                    perm=tuple(((w, (w + 1) % lower) for w in range(lower))),
+                )
+                n_now = lax.dynamic_update_slice_in_dim(
+                    n_now, arr_out, (w2 - dev_i) % lower * opened, axis=1
+                )
+                if 2 * dev_i < lower:
+                    even = jax.lax.ppermute(
+                        even,
+                        axis_name=lane_axis,
+                        perm=tuple(((w, (w - 1) % lower) for w in range(lower))),
+                    )
+                    n_now = lax.dynamic_update_slice_in_dim(
+                        n_now, even, (w2 + dev_i) % lower * opened, axis=1
+                    )
+            return n_now
+
         gathered = (
             lax.all_gather(norm_gain, "shard", axis=0, tiled=True),
-            lax.all_gather(w_in, "shard", axis=1, tiled=True),
+            prepare_forms(w_in, "shard"),
             lax.all_gather(conv_weight, "shard", axis=1, tiled=True),
             lax.all_gather(conv_bias, "shard", axis=0, tiled=True),
             lax.all_gather(x_proj, "shard", axis=1, tiled=True),

time: 2380 us -> 2700 us (1.13)
  other arithmetic: 841 us -> 966 us
  blocking collectives: 164 us -> 265 us
  local copies, waits for them, and re-layouts: 197 us -> 266 us
    ppermute x0 -> x3, waiting for transfers between devices: none -> 268 us  [the longest x2 268 us: prepare_forms(): jax.lax.ppermute(arr_out, axis_name=lane_axis, perm=tuple(((w, (w + 1) %...]
    all_gather x1 -> x0, waiting for transfers between devices: 172 us -> none  [body(): lax.all_gather(w_in, 'shard', axis=1, tiled=True)]
    all_gather x1, blocking collectives: 6.11 us -> 103 us  [body(): lax.all_gather(norm_gain, 'shard', axis=0, tiled=True)]
    mul x128, other arithmetic: 0.74 us -> 93.2 us  [block_product(): rate_blk[t] * conv_blk[t]]
    all_gather x1, waiting for transfers between devices: 69.6 us -> 0.01 us  [body(): lax.all_gather(out_proj, 'shard', axis=1, tiled=True)]
    dynamic_update_slice x0 -> x4, local copies, waits for them, and re-layouts: none -> 32.9 us  [the longest x2 16.5 us: prepare_forms(): lax.dynamic_update_slice_in_dim(n_now, arr_out, (w2 - dev_i) % lower * op...]
    mul x32, other arithmetic: 20.4 us -> 48.3 us  [decay_of(): return (1.0 - rate_row[:, None] * (key_row * key_row)[None, :]) * keep_val]
  transfers between devices with their start and end apart: 19 -> 21, of which waited for: 10 -> 7; matrix products, arithmetic and copies ran while one was open for 39% -> 35% of each run, Pallas kernels for 0% -> 0%
where the time goes in v1:
time: 2700 us; the launch traced here: 2670 us
  other arithmetic  966 us (36%)
  waiting for transfers between devices  909 us (34%)
  local copies, waits for them, and re-layouts  266 us (10%)
  blocking collectives  265 us (10%)
  matrix products  221 us (8%)
    reduce_scatter x1, waiting for transfers between devices, body(): lax.psum_scatter(shard_sums[1], 'replica', scatter_dimension=0, tiled=True)  286 us
    ppermute x2, waiting for transfers between devices, prepare_forms(): jax.lax.ppermute(arr_out, axis_name=lane_axis, perm=tuple(((w, (w + 1) %...  268 us
    reduce_scatter x1, waiting for transfers between devices, body(): lax.psum_scatter(full_sums[1].astype(jnp.bfloat16), 'shard', scatter_dime...  231 us
    reduce_sum x72, other arithmetic, decay_of(): return (1.0 - rate_row[:, None] * (key_row * key_row)[None, :]) * keep_val  209 us
    reduce_sum x72, other arithmetic, block_forward(): outputs.append(jnp.sum(carried * query_blk[t][None, :], axis=1))  157 us
    all_gather x1, blocking collectives, body(): lax.all_gather(norm_gain, 'shard', axis=0, tiled=True)  103 us
    psum x1, blocking collectives, body(): lax.psum((shard_sums[0], shard_sums[2], shard_sums[3], shard_sums[4], sha...  98.9 us
    add x8, other arithmetic, block_product(): decay_now * local_state  98.8 us
  transfers between devices with their start and end apart: 21, of which 7 were waited for; matrix products, arithmetic and copies ran while one was open for 35% of the time, Pallas kernels for 0%

profile of v1, /device:TPU:0, one launch (start us, length us, event | category | flops | bytes accessed | tf_op | source)
XLA Modules:
  0.0 2665.4 jit_solution(10485150160712981154)
XLA Ops:
  10.5 268.5 %collective-permute-done = bf16[2048,2048]{1,0:T(8,128)(2,1)} collective-permute-done((bf16[2048,2048]{1,0:T(8,128)(2,1)}, bf16[2048,2048]{1,0:T(8,128)(2,1)}, u32[]{:S(2)}, u32[]{:S(2)}) %collective-permute-start) | collective-permute-done | bytes 8388640 | tf_op jit(solution)/shard_map/ppermute | solution.py:298
  283.1 102.5 %all-gather.8 = bf16[4,1,512]{2,1,0:T(2,128)(2,1)S(1)} all-gather(bf16[1,1,512]{2,1,0:T(2,128)(2,1)S(1)} %reshape.7362), channel_id=1, replica_groups=mesh['replica'=8,'shard'=4] {'shard'}, dimensions={0}, use_global_device_ids=true | all-gather | bytes 5120 | tf_op jit(solution)/shard_map/all_gather | solution.py:318
  412.5 10.9 broadcast.551
  456.4 13.8 convolution_convert_fusion.1
  472.5 13.8 convolution_convert_fusion
  493.6 15.2 multiply_reduce_fusion.193
  514.6 160.4 %while.190 = (s32[]{:T(128)}, f32[4096,16]{0,1:T(8,128)S(1)}, f32[4096,16]{0,1:T(8,128)}, f32[4,16,4096]{2,1,0:T(8,128)S(1)}, f32[4,16,16]{2,1,0:T(8,128)}, /*in...) while((s32[]{:T(128)}, f32[4096,16]{0,1:T(8,128)S(1)}, ...), condition=%wide.region_3.4_spmd.clone, body=%wide.region_2.3_spmd.clone.sunk | while | flops 10682642 | bytes 3677088 | solution.py:186
  519.0 11.3 fusion.699
  542.0 12.5 multiply_add_fusion.148
  559.0 11.3 fusion.699
  581.9 12.7 multiply_add_fusion.148
  599.1 11.3 fusion.699
  622.1 12.7 multiply_add_fusion.148
  639.3 11.3 fusion.699
  662.2 12.7 multiply_add_fusion.148
  676.1 77.7 %while.194 = (s32[]{:T(128)}, f32[4096,16]{0,1:T(8,128)}, f32[4,16,4096]{2,1,0:T(8,128)S(1)}, f32[4,16,16]{2,1,0:T(8,128)}, f32[4,16]{1,0:T(4,128)}, /*index=5*/...) while((s32[]{:T(128)}, f32[4096,16]{0,1:T(8,128)}, ...), condition=%wide.region_49.50_spmd.clone, body=%wide.region_48.49_spmd.clone.sunk | while | flops 6357267 | bytes 2104179 | solution.py:204
  682.7 12.6 add_multiply_fusion.4
  701.9 12.8 add_multiply_fusion.4
  721.4 12.8 add_multiply_fusion.4
  741.0 12.8 add_multiply_fusion.4
  753.7 15.4 multiply_reduce_fusion.192
  774.7 167.5 %while.192 = (s32[]{:T(128)}, f32[4096,16]{0,1:T(8,128)S(1)}, f32[4096,16]{0,1:T(8,128)S(1)}, f32[4,16,4096]{2,1,0:T(8,128)S(1)}, f32[4,16,16]{2,1,0:T(8,128)}, ...) while((s32[]{:T(128)}, f32[4096,16]{0,1:T(8,128)S(1)}, ...), condition=%wide.region_27.28_spmd.clone, body=%wide.region_26.27_spmd.clone.sunk | while | flops 10682642 | bytes 3677088 | solution.py:186
  781.3 11.5 fusion.703
  804.5 12.0 multiply_add_fusion.149
  823.1 11.5 fusion.703
  846.3 12.0 multiply_add_fusion.149
  864.9 11.5 fusion.703
  888.1 12.0 multiply_add_fusion.149
  907.0 11.5 fusion.703
  930.2 12.0 multiply_add_fusion.149
  942.9 74.7 %while.195 = (s32[]{:T(128)}, f32[4096,16]{0,1:T(8,128)S(1)}, f32[4,16,4096]{2,1,0:T(8,128)S(1)}, f32[4,16,16]{2,1,0:T(8,128)}, f32[4,16]{1,0:T(4,128)}, /*index...) while((s32[]{:T(128)}, f32[4096,16]{0,1:T(8,128)S(1)}, ...), condition=%wide.region_137.138_spmd.clone, body=%wide.region_136.137_spmd.clone.sunk | while | flops 6357267 | bytes 2104179 | solution.py:204
  949.9 11.9 add_multiply_fusion.5
  968.3 11.9 add_multiply_fusion.5
  987.1 11.9 add_multiply_fusion.5
  1005.7 11.9 add_multiply_fusion.5
  1063.5 12.3 while.191
  1077.9 122.3 %while.184 = (s32[]{:T(128)}, f32[4096,16]{0,1:T(8,128)S(1)}, f32[4,4096,16]{1,2,0:T(8,128)}, f32[4,16,4096]{2,1,0:T(8,128)}, f32[4,16,4096]{2,1,0:T(8,128)S(1)}...) while((s32[]{:T(128)}, f32[4096,16]{0,1:T(8,128)S(1)}, ...), condition=%wide.region_23.24_spmd, body=%wide.region_6.23_spmd.sunk | while | flops 11534609 | bytes 8923085 | solution.py:190
  1086.2 11.7 multiply_reduce_fusion.240
  1116.7 11.7 multiply_reduce_fusion.240
  1147.2 11.7 multiply_reduce_fusion.240
  1177.7 11.7 multiply_reduce_fusion.240
  1202.3 198.0 %while.187 = (s32[]{:T(128)}, f32[4096,16]{0,1:T(8,128)S(1)}, f32[4,16,4096]{2,1,0:T(8,128)}, f32[4,16,4096]{2,1,0:T(8,128)}, f32[4,16,16]{2,1,0:T(8,128)S(1)}, ...) while((s32[]{:T(128)}, f32[4096,16]{0,1:T(8,128)S(1)}, ...), condition=%wide.region_133.134_spmd, body=%wide.region_52.133_spmd.sunk | while | flops 34942480 | bytes 21260876 | solution.py:209
  1209.4 10.4 multiply_add_fusion.146
  1258.6 10.4 multiply_add_fusion.146
  1308.3 10.4 multiply_add_fusion.146
  1357.4 10.4 multiply_add_fusion.146
  1415.8 103.9 %while.185 = (s32[]{:T(128)}, f32[4096,16]{0,1:T(8,128)S(1)}, f32[4,4096,16]{1,2,0:T(8,128)}, f32[4,16,4096]{2,1,0:T(8,128)}, f32[4,16,4096]{2,1,0:T(8,128)S(1)}...) while((s32[]{:T(128)}, f32[4096,16]{0,1:T(8,128)S(1)}, ...), condition=%wide.region_47.48_spmd, body=%wide.region_30.47_spmd.sunk | while | flops 11534609 | bytes 8923085 | solution.py:190
  1422.9 11.8 multiply_reduce_fusion.249
  1448.8 11.8 multiply_reduce_fusion.249
  1474.7 11.8 multiply_reduce_fusion.249
  1500.8 11.8 multiply_reduce_fusion.249
  1521.9 191.8 %while.189 = (s32[]{:T(128)}, f32[4096,16]{0,1:T(8,128)S(1)}, f32[4,16,4096]{2,1,0:T(8,128)}, f32[4,16,4096]{2,1,0:T(8,128)}, f32[4,16,16]{2,1,0:T(8,128)S(1)}, ...) while((s32[]{:T(128)}, f32[4096,16]{0,1:T(8,128)S(1)}, ...), condition=%wide.region_221.222_spmd, body=%wide.region_140.221_spmd.sunk | while | flops 34942480 | bytes 21260876 | solution.py:209
  1720.3 13.3 fusion.432
  1733.6 18.9 add_convert_fusion.1
  1769.4 26.4 fusion.425
  1795.8 34.0 %add_convert_fusion = bf16[2048,8192]{1,0:T(8,128)(2,1)} fusion(f32[2048,8192]{1,0:T(8,128)} %fusion.425, bf16[64,4096]{1,0:T(8,128)(2,1)S(1)} %copy-done.24, bf16[3,4096]{1,0:T(4,128)(2,1)S(1)} %fusion.445, bf16[61,4096]{1,0:T(8,128)(2,1)S(1)} %slice.5301, f32[64]{0:T(128)S(1)} %copy-done.55, f32[2048]{0:T(1024)S(1)} %bitcast.3491, ...), kind=kOutput, calls=%fused_computation.1428 | convolution fusion | flops 2184708096 | bytes 102015488 | tf_op jit(solution)/shard_map/dot_general | solution.py:59
  1838.9 39.9 %reduce-scatter.18.cloned.1.call-done = bf16[4096,512]{1,0:T(8,128)(2,1)} async-done(((bf16[4096,2048]{1,0:T(8,128)(2,1)}), bf16[4096,512]{1,0:T(8,128)(2,1)}) %reduce-scatter.18.cloned.1.call-update) | async-done | bytes 4194320 | tf_op jit(solution)/shard_map/reduce_scatter | solution.py:361
  1885.7 230.7 %reduce-scatter.10.cloned.1.call-done = bf16[2048,2048]{1,0:T(8,128)(2,1)} async-done(((bf16[2048,8192]{1,0:T(8,128)(2,1)}), bf16[2048,2048]{1,0:T(8,128)(2,1)}) %reduce-scatter.10.cloned.1.call-update) | async-done | bytes 8388624 | tf_op jit(solution)/shard_map/reduce_scatter | solution.py:340
  2116.4 11.6 convert_element_type.346
  2149.5 15.9 fusion.424
  2165.4 15.9 fusion.419
  2200.4 98.9 %all-reduce.216 = (f32[512]{0:T(512)}, f32[4,1024]{1,0:T(4,128)}, f32[1024]{0:T(1024)}, f32[160,1024]{1,0:T(8,128)}, f32[128,1024]{1,0:T(8,128)}, /*index=5*/f32[1024]{0:T(1024)}, f32[1024]{0:T(1024)}) all-reduce(f32[512]{0:T(512)S(1)} %dynamic-slice_convert_fusion.3, ...), channel_id=1, replica_groups=mesh['replica'=8,'shard'=4] {'replica'}, use_global_device_ids=true, to_apply=%region_227.228 | all-reduce | flops 302592 | bytes 1822720 | tf_op jit(solution)/shard_map/psum | solution.py:369
  2299.3 73.4 %reduce-scatter.20.cloned.1.call-done = f32[512,512]{1,0:T(8,128)} async-done(((f32[4096,512]{1,0:T(8,128)}), f32[512,512]{1,0:T(8,128)}) %reduce-scatter.20.cloned.1.call-update) | async-done | bytes 1048592 | tf_op jit(solution)/shard_map/reduce_scatter | solution.py:367
  2372.8 285.7 %reduce-scatter.12.cloned.1.call-done = f32[256,2048]{1,0:T(8,128)} async-done(((f32[2048,2048]{1,0:T(8,128)}), f32[256,2048]{1,0:T(8,128)}) %reduce-scatter.12.cloned.1.call-update) | async-done | bytes 2097168 | tf_op jit(solution)/shard_map/reduce_scatter | solution.py:366
  (1395 shorter events, 926.9 us)
Async XLA Ops:
  7.2 275.9 %copy-start.86 = (bf16[512]{0:T(512)(128)(2,1)S(1)}, bf16[512]{0:T(512)(128)(2,1)}, u32[]{:S(2)}) copy-start(bf16[512]{0:T(512)(128)(2,1)} %param.38) | copy-start | bytes 3076
  7.2 378.4 %copy-start.82 = (bf16[1024]{0:T(1024)(128)(2,1)S(1)}, bf16[1024]{0:T(1024)(128)(2,1)}, u32[]{:S(2)}) copy-start(bf16[1024]{0:T(1024)(128)(2,1)} %param.41) | copy-start | bytes 6148
  7.2 386.6 %copy-start.83 = (bf16[1024]{0:T(1024)(128)(2,1)S(1)}, bf16[1024]{0:T(1024)(128)(2,1)}, u32[]{:S(2)}) copy-start(bf16[1024]{0:T(1024)(128)(2,1)} %param.45) | copy-start | bytes 6148
  7.2 392.5 %copy-start.84 = (bf16[1024]{0:T(1024)(128)(2,1)S(1)}, bf16[1024]{0:T(1024)(128)(2,1)}, u32[]{:S(2)}) copy-start(bf16[1024]{0:T(1024)(128)(2,1)} %param.44) | copy-start | bytes 6148
  7.2 397.7 %copy-start.85 = (s32[2,256]{1,0:T(2,128)S(1)}, s32[2,256]{1,0:T(2,128)}, u32[]{:S(2)}) copy-start(s32[2,256]{1,0:T(2,128)} %param.37) | copy-start | bytes 6148
  7.2 399.1 %copy-start.77 = (bf16[4,1024]{1,0:T(4,128)(2,1)S(1)}, bf16[4,1024]{1,0:T(4,128)(2,1)}, u32[]{:S(2)}) copy-start(bf16[4,1024]{1,0:T(4,128)(2,1)} %param.40) | copy-start | bytes 24580
  7.2 404.3 %copy-start.1 = (bf16[2,64,2048]{2,1,0:T(8,128)(2,1)S(1)}, bf16[2,64,2048]{2,1,0:T(8,128)(2,1)}, u32[]{:S(2)}) copy-start(bf16[2,64,2048]{2,1,0:T(8,128)(2,1)} %param.36) | copy-start | bytes 1572868
  7.3 486.3 %all-gather.21.cloned.1.call-start = ((), (), s32[]{:S(2)}) async-start(), calls=%async_computation.9 | async-start | bytes 20971520 | tf_op jit(solution)/shard_map/all_gather | solution.py:326
  8.0 500.9 %all-gather.17.cloned.1.call-start = ((), (), s32[]{:S(2)}) async-start(), calls=%async_computation.7 | async-start | bytes 1638400 | tf_op jit(solution)/shard_map/all_gather | solution.py:322
  8.0 271.0 %collective-permute-start = (bf16[2048,2048]{1,0:T(8,128)(2,1)}, bf16[2048,2048]{1,0:T(8,128)(2,1)}, u32[]{:S(2)}, u32[]{:S(2)}) collective-permute-start(bf16[2048,2048]{1,0:T(8,128)(2,1)} %param.39), channel_id=1, source_target_pairs={{0,1},{1,2},{2,3},{3,0},{4,5},{5,6},{6,7},{7,4},{8,9},{9,10},{10,1... | collective-permute-start | bytes 25165832 | tf_op jit(solution)/shard_map/ppermute | solution.py:298
  8.5 431.4 %collective-permute-start.1 = (bf16[2048,2048]{1,0:T(8,128)(2,1)}, bf16[2048,2048]{1,0:T(8,128)(2,1)}, u32[]{:S(2)}, u32[]{:S(2)}) collective-permute-start(bf16[2048,2048]{1,0:T(8,128)(2,1)} %param.39), channel_id=1, source_target_pairs={{0,3},{1,0},{2,1},{3,2},{4,7},{5,4},{6,5},{7,6},{8,11},{9,8},{10,9... | collective-permute-start | bytes 25165832 | tf_op jit(solution)/shard_map/ppermute | solution.py:307
  279.0 169.1 %collective-permute-start.2 = (bf16[2048,2048]{1,0:T(8,128)(2,1)}, bf16[2048,2048]{1,0:T(8,128)(2,1)}, u32[]{:S(2)}, u32[]{:S(2)}) collective-permute-start(bf16[2048,2048]{1,0:T(8,128)(2,1)} %collective-permute-done), channel_id=1, source_target_pairs={{0,1},{1,2},{2,3},{3,0},{4,5},{5,6},{6,7},{7,4},{8,9},{9,10},{10,1... | collective-permute-start | bytes 25165832 | tf_op jit(solution)/shard_map/ppermute | solution.py:298
  281.6 230.2 %all-gather.19.cloned.1.call-start = ((), (), s32[]{:S(2)}) async-start(), calls=%async_computation.8 | async-start | bytes 1310720 | tf_op jit(solution)/shard_map/all_gather | solution.py:323
  282.3 775.3 %all-gather.23.cloned.1.call-start = ((), (), s32[]{:S(2)}) async-start(), calls=%async_computation.16 | async-start | bytes 1310720 | tf_op jit(solution)/shard_map/all_gather | solution.py:19
  282.5 140.9 %copy-start.50 = (bf16[4,16,16]{2,1,0:T(8,128)(2,1)}, bf16[4,16,16]{2,1,0:T(8,128)(2,1)S(1)}, u32[]{:S(2)}) copy-start(bf16[4,16,16]{2,1,0:T(8,128)(2,1)S(1)} %fusion.626) | copy-start | bytes 6148
  385.6 86.8 %copy-start.39 = (f32[4,1,512]{2,1,0:T(1,128)}, f32[4,1,512]{2,1,0:T(1,128)S(1)}, u32[]{:S(2)}) copy-start(f32[4,1,512]{2,1,0:T(1,128)S(1)} %convert_element_type.375) | copy-start | bytes 24580
  393.8 99.7 %copy-start.64 = (f32[4096]{0:T(1024)}, f32[4096]{0:T(1024)S(1)}, u32[]{:S(2)}) copy-start(f32[4096]{0:T(1024)S(1)} %convert_element_type.292) | copy-start | bytes 49156
  404.9 106.9 %copy-start.62 = (f32[4096]{0:T(1024)}, f32[4096]{0:T(1024)S(1)}, u32[]{:S(2)}) copy-start(f32[4096]{0:T(1024)S(1)} %convert_element_type.305) | copy-start | bytes 49156
  411.8 44.6 %copy-start.56 = (f32[64]{0:T(128)}, f32[64]{0:T(128)S(1)}, u32[]{:S(2)}) copy-start(f32[64]{0:T(128)S(1)} %add_rsqrt_fusion.1) | copy-start | bytes 772
  411.8 60.7 %copy-start.54 = (f32[64]{0:T(128)}, f32[64]{0:T(128)S(1)}, u32[]{:S(2)}) copy-start(f32[64]{0:T(128)S(1)} %add_rsqrt_fusion) | copy-start | bytes 772
  412.5 81.1 %copy-start.87 = (f32[64]{0:T(128)}, f32[64]{0:T(128)S(1)}, u32[]{:S(2)}) copy-start(f32[64]{0:T(128)S(1)} %get-tuple-element.3214) | copy-start | bytes 772
  412.5 81.1 %copy-start.89 = (f32[64]{0:T(128)}, f32[64]{0:T(128)S(1)}, u32[]{:S(2)}) copy-start(f32[64]{0:T(128)S(1)} %get-tuple-element.3217) | copy-start | bytes 772
  412.5 81.1 %copy-start.91 = (f32[64]{0:T(128)}, f32[64]{0:T(128)S(1)}, u32[]{:S(2)}) copy-start(f32[64]{0:T(128)S(1)} %get-tuple-element.3218) | copy-start | bytes 772
  431.7 61.9 %copy-start.69 = (f32[1,4096]{1,0:T(1,128)}, f32[1,4096]{1,0:T(1,128)S(1)}, u32[]{:S(2)}) copy-start(f32[1,4096]{1,0:T(1,128)S(1)} %get-tuple-element.3206) | copy-start | bytes 49156
  431.7 61.9 %copy-start.71 = (f32[1,4096]{1,0:T(1,128)}, f32[1,4096]{1,0:T(1,128)S(1)}, u32[]{:S(2)}) copy-start(f32[1,4096]{1,0:T(1,128)S(1)} %get-tuple-element.3207) | copy-start | bytes 49156
  431.7 61.9 %copy-start.73 = (f32[1,4096]{1,0:T(1,128)}, f32[1,4096]{1,0:T(1,128)S(1)}, u32[]{:S(2)}) copy-start(f32[1,4096]{1,0:T(1,128)S(1)} %get-tuple-element.3208) | copy-start | bytes 49156
  431.7 61.9 %copy-start.75 = (f32[1,4096]{1,0:T(1,128)}, f32[1,4096]{1,0:T(1,128)S(1)}, u32[]{:S(2)}) copy-start(f32[1,4096]{1,0:T(1,128)S(1)} %get-tuple-element.3209) | copy-start | bytes 49156
  470.2 23.4 copy-start.32
  470.2 21.0 collective-permute-start.3
  486.3 7.3 copy-start.36
  487.3 5.1 collective-permute-start.4
  675.7 384.8 %all-gather.25.cloned.1.call-start = ((), (), s32[]{:S(2)}) async-start(), calls=%async_computation.17 | async-start | bytes 1310720 | tf_op jit(solution)/shard_map/all_gather | solution.py:19
  942.2 95.5 %copy-start.5 = (f32[4096,16]{0,1:T(8,128)}, f32[4096,16]{0,1:T(8,128)S(1)}, u32[]{:S(2)}) copy-start(f32[4096,16]{0,1:T(8,128)S(1)} %get-tuple-element.1341) | copy-start | bytes 786436
  942.9 74.7 %copy-start.7 = (f32[4096,16]{0,1:T(8,128)S(1)}, f32[4096,16]{0,1:T(8,128)}, u32[]{:S(2)}) copy-start(f32[4096,16]{0,1:T(8,128)} %copy-done.6) | copy-start | bytes 786436
  1017.6 16.7 copy-start.8
  1017.6 8.6 copy-start.10
  1034.4 365.9 %all-gather.27.cloned.1.call-start = ((), (), s32[]{:S(2)}) async-start(), calls=%async_computation.18 | async-start | bytes 1310720 | tf_op jit(solution)/shard_map/all_gather | solution.py:19
  1034.5 10.7 copy-start.9
  1054.2 349.1 %all-gather.29.cloned.1.call-start = ((), (), s32[]{:S(2)}) async-start(), calls=%async_computation.19 | async-start | bytes 1310720 | tf_op jit(solution)/shard_map/all_gather | solution.py:19
  1057.6 821.2 %reduce-scatter.18.cloned.1.call-start = ((), (), s32[]{:S(2)}) async-start(), calls=%async_computation.14 | async-start | bytes 20971520 | tf_op jit(solution)/shard_map/reduce_scatter | solution.py:361
  1301.3 7.0 copy-start.3
  1521.9 191.8 %copy-start.14 = (bf16[64,4096]{1,0:T(8,128)(2,1)S(1)}, bf16[64,4096]{1,0:T(8,128)(2,1)}, u32[]{:S(2)}) copy-start(bf16[64,4096]{1,0:T(8,128)(2,1)} %copy-done.13) | copy-start | bytes 1572868
  1521.9 191.9 %copy-start.53 = (f32[4096]{0:T(1024)S(1)}, f32[4096]{0:T(1024)}, u32[]{:S(2)}) copy-start(f32[4096]{0:T(1024)} %convert_element_type.309) | copy-start | bytes 49156
  1665.8 6.7 copy-start.4
  1720.3 13.3 copy-start.17
  1720.3 13.3 copy-start.19
  1752.5 363.9 %reduce-scatter.10.cloned.1.call-start = ((), (), s32[]{:S(2)}) async-start(), calls=%async_computation.10 | async-start | bytes 41943040 | tf_op jit(solution)/shard_map/reduce_scatter | solution.py:340
  1760.1 6.8 collective-permute-start.6
  1765.3 30.4 %copy-start.28 = (bf16[61,4096]{1,0:T(8,128)(2,1)}, bf16[61,4096]{1,0:T(8,128)(2,1)S(1)}, u32[]{:S(2)}) copy-start(bf16[61,4096]{1,0:T(8,128)(2,1)S(1)} %slice.5301) | copy-start | bytes 1499140
  1765.5 30.2 %copy-start.26 = (bf16[61,4096]{1,0:T(8,128)(2,1)}, bf16[61,4096]{1,0:T(8,128)(2,1)S(1)}, u32[]{:S(2)}) copy-start(bf16[61,4096]{1,0:T(8,128)(2,1)S(1)} %slice.5298) | copy-start | bytes 1499140
  1765.5 3.8 collective-permute-start.5
  1769.3 26.4 copy-start.24
  1769.3 26.4 copy-start.55
  1829.8 363.3 %reduce-scatter.22.cloned.1.call-start = ((), (), s32[]{:S(2)}) async-start(), calls=%async_computation.20 | async-start | bytes 1310720
  1833.5 360.6 %reduce-scatter.16.cloned.1.call-start = ((), (), s32[]{:S(2)}) async-start(), calls=%async_computation.13 | async-start | bytes 1310720 | tf_op jit(solution)/shard_map/reduce_scatter | solution.py:352
  1836.1 364.3 %reduce-scatter.14.cloned.1.call-start = ((), (), s32[]{:S(2)}) async-start(), calls=%async_computation.12 | async-start | bytes 1638400 | tf_op jit(solution)/shard_map/reduce_scatter | solution.py:349
  1838.8 533.9 %reduce-scatter.20.cloned.1.call-start = ((), (), s32[]{:S(2)}) async-start(), calls=%async_computation.15 | async-start | bytes 9437184 | tf_op jit(solution)/shard_map/reduce_scatter | solution.py:367
  1885.4 773.1 %reduce-scatter.12.cloned.1.call-start = ((), (), s32[]{:S(2)}) async-start(), calls=%async_computation.11 | async-start | bytes 18874368 | tf_op jit(solution)/shard_map/reduce_scatter | solution.py:366
  2130.6 9.1 copy-start.18
  2139.7 9.8 copy-start.25
  2139.7 9.8 copy-start.29
  2149.5 15.9 copy-start.23
  2149.5 15.9 copy-start.27
  2165.4 26.4 copy-start.38
  (62 other events, 199.4 us)
Sparse Core Ops, SparseCore 0:
  9.6 198.6 all-gather.20
  281.7 23.4 all-gather.16
  306.8 19.5 all-gather.18
  675.8 17.6 all-gather.22
  1034.5 17.5 all-gather.24
  1054.3 16.7 all-gather.26
  1072.7 16.7 all-gather.28
  1752.7 126.0 reduce-scatter.17
  1881.5 234.7 reduce-scatter.9
  2118.9 24.8 reduce-scatter.21
  2146.4 24.8 reduce-scatter.15
  2173.8 26.5 reduce-scatter.13
  2204.6 168.1 reduce-scatter.19
  2377.4 281.0 reduce-scatter.11
